TPU v7x, 32 devices: a whole 2x2x4 slice. The times are simulated.
32 devices in a mesh: lat: 4 (over z), lon: 8 (over y, x, core).
Axes of the slice: x: 2, y: 2, z: 4, core: 2. Of those that a mesh axis runs over, the one named last changes fastest.
Arguments:
- state: bfloat16 [192, 64, 1024], P(None, 'lat', 'lon'), may hold values from -6 to 6
- depth_kernel: bfloat16 [192, 7, 7], replicated, may hold values from -0.875 to 0.875
- point_weight: bfloat16 [192, 192], replicated, may hold values from -0.4375 to 0.4375
- column_index: int32 [16384, 4], P(('lat', 'lon')), may hold values from 0 to 2047, as said below
- column_weight: bfloat16 [16384, 4], P(('lat', 'lon')), may hold values from 0.049804688 to 0.59765625
- owner: int32 [16384, 1], P(('lat', 'lon')), may hold values from 0 to 7; in each aligned block of 512 rows (0 to 511, 512 to 1023, ...) at most 64 rows name the same one
- observed: bfloat16 [16384, 137], P(('lat', 'lon')), may hold values from -6 to 6
- hidden_weight: bfloat16 [8, 192, 512], P('lon'), may hold values from -0.4375 to 0.4375
- level_weight: bfloat16 [8, 512, 137], P('lon'), may hold values from -0.25 to 0.25
- inverse_error: bfloat16 [8, 137], P('lon'), may hold values from 0.25 to 4
Outputs:
- gradient: bfloat16 [192, 64, 1024], P(None, 'lat', 'lon')
- departures: bfloat16 [16384, 137], P(('lat', 'lon'))
Inputs may be any that keep to these rules, and one draw needn't show every extreme that they name: `column_index`: the four columns of one grid box of the sounding's own tile: b, b + 1, b + 128, b + 129. `owner`: among the 512 soundings of one tile no instrument appears more than 64 times.
All inputs are finite; a program needn't handle non-finite values.
Results may differ from a plain program's by a relative error of at most 0.0085.
Values may be sent and summed in bfloat16 or wider, within the bound.
A program may use at most 128 MiB of HBM per device.

v0:
```python
import jax
import jax.numpy as jnp
from jax import lax
from jax.experimental import pallas as pl
from jax.experimental.pallas import tpu as pltpu
from jax.sharding import PartitionSpec as P

CAP = 64
F32 = jnp.float32
BF = jnp.bfloat16
VM = pl.BlockSpec(memory_space=pltpu.VMEM)


def nn(a, b):
    return jnp.dot(a, b, preferred_element_type=F32)


def nt(a, b):
    return lax.dot_general(a, b, (((1,), (1,)), ((), ())), preferred_element_type=F32)


def call(kernel, out_shape, scratch, flops, nbytes, *args):
    return pl.pallas_call(
        kernel,
        out_shape=out_shape,
        in_specs=[VM] * len(args),
        out_specs=jax.tree.map(lambda _: VM, out_shape),
        scratch_shapes=scratch,
        cost_estimate=pl.CostEstimate(flops=flops, bytes_accessed=nbytes, transcendentals=0),
        compiler_params=pltpu.CompilerParams(vmem_limit_bytes=56 << 20),
    )(*args)


def conv_group(x_ref, h_ref, k_ref, base, flip):
    rows = x_ref.shape[0]
    breadth = x_ref.shape[2]
    height = rows - 6
    lane = lax.broadcasted_iota(jnp.int32, (16, breadth), 1)
    taps = k_ref[pl.ds(base, 16), :]
    acc = [None] * height
    for col in range(7):
        shift = col - 3
        weights = []
        for row in range(7):
            t = (6 - row) * 7 + 6 - col if flip else row * 7 + col
            weights.append(jnp.broadcast_to(taps[:, t : t + 1], (16, breadth)))
        for r in range(rows):
            v = x_ref[r, pl.ds(base, 16), :].astype(F32)
            if shift:
                edge = h_ref[r, pl.ds(base, 16), :].astype(F32)
                mask = lane < shift if shift > 0 else lane >= breadth + shift
                v = pltpu.roll(jnp.where(mask, edge, v), (-shift) % breadth, 1)
            for row in range(7):
                i = r - row
                if 0 <= i < height:
                    term = weights[row] * v
                    acc[i] = term if acc[i] is None else acc[i] + term
    return acc


def prep_kernel(owner_row, owner_col, row0, col0, w_ref, obs_ref, wt_ref, p_ref, pt_ref, obs_slot):
    height, obs, breadth = wt_ref.shape
    slots = p_ref.shape[0]
    n = slots // CAP
    lane = lax.broadcasted_iota(jnp.int32, (obs, breadth), 1)
    c0 = jnp.broadcast_to(col0[...], (obs, breadth))
    r0 = jnp.broadcast_to(row0[...], (obs, breadth))
    w = w_ref[...].astype(F32)
    zero = jnp.zeros((obs, breadth), F32)
    first = lane == c0
    second = lane == c0 + 1
    top = jnp.where(first, w[:, 0:1], jnp.where(second, w[:, 1:2], zero))
    bottom = jnp.where(first, w[:, 2:3], jnp.where(second, w[:, 3:4], zero))
    for r in range(height):
        wt_ref[r] = jnp.where(r0 == r, top, jnp.where(r0 == r - 1, bottom, zero)).astype(BF)
    si = lax.broadcasted_iota(jnp.int32, (obs, obs), 0)
    sj = lax.broadcasted_iota(jnp.int32, (obs, obs), 1)
    ones_u = jnp.where(si < sj, 1.0, 0.0).astype(BF)
    ones_l = jnp.where(sj < si, 1.0, 0.0).astype(BF)
    own = owner_row[...]
    hot = jnp.where(lax.broadcasted_iota(jnp.int32, (n, obs), 0) == own, 1.0, 0.0)
    within = jnp.sum(nn(hot.astype(BF), ones_u) * hot, axis=0, keepdims=True)
    slot_row = own * CAP + within.astype(jnp.int32)
    place = lax.broadcasted_iota(jnp.int32, (slots, obs), 0) == slot_row
    p = jnp.where(place, 1.0, 0.0).astype(BF)
    p_ref[...] = p
    own = owner_col[...]
    hot = jnp.where(lax.broadcasted_iota(jnp.int32, (obs, 128), 1) == own, 1.0, 0.0)
    within = jnp.sum(nn(ones_l, hot.astype(BF)) * hot, axis=1, keepdims=True)
    slot_col = own * CAP + within.astype(jnp.int32)
    place = lax.broadcasted_iota(jnp.int32, (obs, slots), 1) == slot_col
    pt_ref[...] = jnp.where(place, 1.0, 0.0).astype(BF)
    obs_slot[...] = nn(p, obs_ref[...]).astype(BF)


def forward_kernel(x_ref, h_ref, k_ref, pwt_ref, wt_ref, p_ref, dg_ref, prof_ref, mixed, total):
    rows, channels, breadth = x_ref.shape
    height = rows - 6

    def group(g, carry):
        base = pl.multiple_of(g * 16, 16)
        for i, v in enumerate(conv_group(x_ref, h_ref, k_ref, base, False)):
            mixed[i, pl.ds(base, 16), :] = v.astype(BF)
        return carry

    lax.fori_loop(0, channels // 16, group, 0)
    total[...] = jnp.zeros_like(total)
    a, b = 0.7978845608028654, 0.044715

    def pair(q, carry):
        r = q * 2
        pre = nn(pwt_ref[...], jnp.concatenate([mixed[r], mixed[r + 1]], axis=1))
        square = pre * pre
        t = jnp.tanh(a * (pre + b * (square * pre)))
        half = 0.5 * (1.0 + t)
        slope = half + (0.5 * pre) * (1.0 - t * t) * (a * (1.0 + (3.0 * b) * square))
        dg_ref[r] = slope[:, :breadth]
        dg_ref[r + 1] = slope[:, breadth:]
        state = jnp.concatenate([x_ref[r + 3], x_ref[r + 4]], axis=1).astype(F32)
        analysis = (state + pre * half).astype(BF)
        total[...] += nt(jnp.concatenate([wt_ref[r], wt_ref[r + 1]], axis=1), analysis)
        return carry

    lax.fori_loop(0, height // 2, pair, 0)
    prof_ref[...] = nn(p_ref[...], total[...].astype(BF)).astype(BF)


def middle_kernel(levels, prof_ref, obs_ref, op_ref, wt_ref, pt_ref, dg_ref, pw_ref, dep_ref, fb_ref, mb_ref, adj, mis):
    height, channels, breadth = dg_ref.shape
    n = op_ref.shape[0]
    err_row = op_ref.shape[1] - 16

    def instrument(o, carry):
        at = pl.ds(pl.multiple_of(o * CAP, CAP), CAP)
        hw = op_ref[o, :channels, :]
        lw = op_ref[o, channels : channels + levels, :]
        err = op_ref[o, err_row : err_row + 1, :levels].astype(F32)
        squashed = jnp.tanh(nn(prof_ref[at, :], hw))
        misfit = nt(squashed.astype(BF), lw) - obs_ref[at, :].astype(F32)
        mis[at, :] = misfit.astype(BF)
        back = nn((err * misfit).astype(BF), lw) * (1.0 - squashed * squashed)
        adj[at, :] = nt(back.astype(BF), hw).astype(BF)
        return carry

    lax.fori_loop(0, n, instrument, 0)
    dep_ref[...] = nn(pt_ref[...], mis[...]).astype(BF)
    adj_t = nn(pt_ref[...], adj[...]).T.astype(BF)

    def pair(q, carry):
        r = q * 2
        fb = nn(adj_t, jnp.concatenate([wt_ref[r], wt_ref[r + 1]], axis=1))
        fb_ref[r] = fb[:, :breadth]
        fb_ref[r + 1] = fb[:, breadth:]
        gate = (fb * jnp.concatenate([dg_ref[r], dg_ref[r + 1]], axis=1)).astype(BF)
        mb = nn(pw_ref[...], gate).astype(BF)
        mb_ref[r] = mb[:, :breadth]
        mb_ref[r + 1] = mb[:, breadth:]
        return carry

    lax.fori_loop(0, height // 2, pair, 0)


def backward_kernel(x_ref, h_ref, k_ref, fb_ref, out_ref):
    channels = x_ref.shape[1]

    def group(g, carry):
        base = pl.multiple_of(g * 16, 16)
        for i, v in enumerate(conv_group(x_ref, h_ref, k_ref, base, True)):
            out_ref[i, pl.ds(base, 16), :] = (v + fb_ref[i, pl.ds(base, 16), :]).astype(BF)
        return carry

    lax.fori_loop(0, channels // 16, group, 0)


def halo(x):
    lat, lon = lax.axis_size("lat"), lax.axis_size("lon")
    up = [(i, i + 1) for i in range(lat - 1)]
    down = [(i + 1, i) for i in range(lat - 1)]
    right = [(i, (i + 1) % lon) for i in range(lon)]
    left = [((i + 1) % lon, i) for i in range(lon)]
    x = jnp.concatenate(
        [lax.ppermute(x[-3:], "lat", up), x, lax.ppermute(x[:3], "lat", down)], axis=0
    )
    rows, channels, breadth = x.shape
    head = lax.ppermute(x[:, :, :3].transpose(2, 0, 1), "lon", left).transpose(1, 2, 0)
    tail = lax.ppermute(x[:, :, -3:].transpose(2, 0, 1), "lon", right).transpose(1, 2, 0)
    edge = jnp.concatenate([head, jnp.zeros((rows, channels, breadth - 6), x.dtype), tail], axis=2)
    return x, edge


def body(
    state,
    depth_kernel,
    point_weight,
    column_index,
    column_weight,
    owner,
    observed,
    hidden_weight,
    level_weight,
    inverse_error,
):
    channels, height, breadth = state.shape
    obs, levels = observed.shape
    hid = hidden_weight.shape[2]
    n = lax.axis_size("lon")
    slots = n * CAP
    sds = jax.ShapeDtypeStruct
    fill = (-(channels + levels)) % 16
    pack = jnp.concatenate(
        [
            hidden_weight[0],
            jnp.pad(level_weight[0].T, ((0, fill), (0, 0))),
            jnp.pad(inverse_error, ((0, 15), (0, hid - levels))),
        ],
        axis=0,
    )
    operators = lax.all_gather(pack[None], "lon", axis=0, tiled=True)
    taps = jnp.pad(depth_kernel.reshape(channels, 49).astype(F32), ((0, 0), (0, 79)))
    x, edge = halo(state.transpose(1, 0, 2))
    row0 = column_index[:, :1] // breadth
    col0 = column_index[:, :1] - row0 * breadth
    wt, p, pt, obs_slot = call(
        prep_kernel,
        (sds((height, obs, breadth), BF), sds((slots, obs), BF), sds((obs, slots), BF), sds((slots, levels), BF)),
        [],
        10**8,
        4 << 20,
        owner.reshape(1, obs),
        owner,
        row0,
        col0,
        column_weight,
        observed,
    )
    slope, prof = call(
        forward_kernel,
        (sds((height, channels, breadth), F32), sds((slots, channels), BF)),
        [pltpu.VMEM((height, channels, breadth), BF), pltpu.VMEM((obs, channels), F32)],
        10**9,
        8 << 20,
        x,
        edge,
        taps,
        point_weight.T,
        wt,
        p,
    )
    departures, fb, mb = call(
        lambda *refs: middle_kernel(levels, *refs),
        (sds((obs, levels), BF), sds((height, channels, breadth), F32), sds((height, channels, breadth), BF)),
        [pltpu.VMEM((slots, channels), BF), pltpu.VMEM((slots, levels), BF)],
        10**9,
        12 << 20,
        prof,
        obs_slot,
        operators,
        wt,
        pt,
        slope,
        point_weight,
    )
    x, edge = halo(mb)
    grad = call(
        backward_kernel,
        sds((height, channels, breadth), BF),
        [],
        10**9,
        8 << 20,
        x,
        edge,
        taps,
        fb,
    )
    return (grad.transpose(1, 0, 2), departures)


def solution(mesh):
    in_specs = (
        P(None, "lat", "lon"),
        P(),
        P(),
        P(("lat", "lon"), None),
        P(("lat", "lon"), None),
        P(("lat", "lon"), None),
        P(("lat", "lon"), None),
        P("lon", None, None),
        P("lon", None, None),
        P("lon", None),
    )
    out_specs = (P(None, "lat", "lon"), P(("lat", "lon"), None))
    return jax.shard_map(body, mesh=mesh, in_specs=in_specs, out_specs=out_specs, check_vma=False)
```

profile of v0, /device:TPU:0, one launch (start us, length us, event | category | flops | bytes accessed | tf_op | source)
XLA Modules:
  0.0 106.3 jit_solution(4121392302877801433)
XLA Ops:
  7.2 1.8 %fusion.4 = bf16[352,512]{1,0:T(8,128)(2,1)} fusion(bf16[1,137]{1,0:T(2,128)(2,1)} %param.19, bf16[137,512]{1,0:T(8,128)(2,1)} %bitcast.35, bf16[192,512]{1,0:T(8,128)(2,1)} %bitcast.34), kind=kLoop, calls=%fused_computation.19 | loop fusion | flops 2162688 | bytes 697618 | tf_op jit(solution)/shard_map/concatenate | solution.py:210
  9.1 0.2 copy.49
  9.4 5.0 %collective-permute-start = (bf16[3,192,128]{2,1,0:T(8,128)(2,1)S(1)}, bf16[3,192,128]{2,1,0:T(8,128)(2,1)S(1)}, u32[]{:S(2)}, u32[]{:S(2)}) collective-permute-start(bf16[3,192,128]{2,1,0:T(8,128)(2,1)S(1)} %get-tuple-element.32), channel_id=1, source_target_pairs={{0,8},{8,16},{16,24},{1,9},{9,17},{17,25},{2,10},{10,18},{18,26},{... | collective-permute-start | bytes 442376 | tf_op jit(solution)/shard_map/ppermute | solution.py:182
  14.3 1.3 %collective-permute-start.1 = (bf16[3,192,128]{2,1,0:T(8,128)(2,1)S(1)}, bf16[3,192,128]{2,1,0:T(8,128)(2,1)S(1)}, u32[]{:S(2)}, u32[]{:S(2)}) collective-permute-start(bf16[3,192,128]{2,1,0:T(8,128)(2,1)S(1)} %get-tuple-element.33), channel_id=1, source_target_pairs={{8,0},{16,8},{24,16},{9,1},{17,9},{25,17},{10,2},{18,10},{26,18},{... | collective-permute-start | bytes 442376 | tf_op jit(solution)/shard_map/ppermute | solution.py:182
  15.6 0.1 copy.47
  15.8 0.1 copy.35
  16.0 1.0 multiply_subtract_fusion
  17.0 0.4 collective-permute-done
  17.4 4.1 %collective-permute-done.1 = bf16[3,192,128]{2,1,0:T(8,128)(2,1)S(1)} collective-permute-done((bf16[3,192,128]{2,1,0:T(8,128)(2,1)S(1)}, bf16[3,192,128]{2,1,0:T(8,128)(2,1)S(1)}, u32[]{:S(2)}, u32[]{:S(2)}) %collective-permute-start.1) | collective-permute-done | bytes 147488 | tf_op jit(solution)/shard_map/ppermute | solution.py:182
  21.5 0.1 pad_maximum_fusion.x_ref
  21.7 0.5 slice_bitcast_fusion.3
  22.2 0.5 copy-done
  22.7 0.5 copy.31
  23.2 0.8 collective-permute-start.2
  24.0 0.5 copy.33
  24.6 0.1 collective-permute-start.3
  24.6 0.6 pad_convert_fusion.k_ref
  25.3 0.9 copy.38.owner_col
  26.1 0.9 copy.40.obs_ref
  27.0 0.8 copy.39.w_ref
  27.8 0.7 copy.36
  28.6 0.1 pad.25.clone
  28.6 4.0 %shard_map.113 = (bf16[16,512,128]{2,1,0:T(8,128)(2,1)}, bf16[512,512]{1,0:T(8,128)(2,1)}, bf16[512,512]{1,0:T(8,128)(2,1)}, bf16[512,137]{1,0:T(8,128)(2,1)}) custom-call(s32[1,512]{1,0:T(1,128)} %bitcast.36, s32[512,1]{1,0:T(8,128)} %copy.38.owner_col, s32[512,1]{1,0:T(8,128)} %get-tuple-element.35.row0, s32[512,1]{1,0:T(8,128)} %get-tuple-element.34.col0, ...), custom_call_target="tpu_custom_call" | custom-call | flops 100000000 | bytes 4194304 | tf_op jit(solution)/shard_map/pallas_call | solution.py:23
  32.7 0.6 copy.32
  33.2 0.6 copy.34
  33.8 1.7 %pad_maximum_fusion.1.h_ref = bf16[22,192,128]{2,1,0:T(8,128)(2,1)} fusion(bf16[22,192,3]{2,1,0:T(8,128)(2,1)S(1)} %bitcast.30, bf16[22,192,3]{2,1,0:T(8,128)(2,1)S(1)} %bitcast.28, bf16[128]{0:T(256)(128)(2,1)S(1)} %pad.25.clone), kind=kLoop, calls=%fused_computation.5 | loop fusion | flops 3244032 | bytes 1132288 | tf_op jit(solution)/shard_map/concatenate | solution.py:187
  35.5 14.9 %shard_map.114 = (f32[16,192,128]{2,1,0:T(8,128)}, bf16[512,192]{1,0:T(8,128)(2,1)}) custom-call(bf16[22,192,128]{2,1,0:T(8,128)(2,1)} %copy-done, bf16[22,192,128]{2,1,0:T(8,128)(2,1)} %pad_maximum_fusion.1.h_ref, f32[192,128]{1,0:T(8,128)} %pad_convert_fusion.k_ref, bf16[192,192]{1,0:T(8,128)(2,1)} %bitcast.33, ...), custom_call_target="tpu_custom_call" | custom-call | flops 1000000000 | bytes 8388608 | tf_op jit(solution)/shard_map/pallas_call | solution.py:23
  50.4 13.1 %shard_map.115 = (bf16[512,137]{1,0:T(8,128)(2,1)}, f32[16,192,128]{2,1,0:T(8,128)}, bf16[16,192,128]{2,1,0:T(8,128)(2,1)}) custom-call(bf16[512,192]{1,0:T(8,128)(2,1)} %get-tuple-element.13.refs_0_, bf16[512,137]{1,0:T(8,128)(2,1)} %get-tuple-element.14.refs_1_, bf16[8,352,512]{2,1,0:T(8,128)(2,1)} %bitcast.32, ...), custom_call_target="tpu_custom_call" | custom-call | flops 1000000000 | bytes 12582912 | tf_op jit(solution)/shard_map/pallas_call | solution.py:23
  63.4 1.1 %fusion.7 = (bf16[3,192,128]{2,1,0:T(8,128)(2,1)S(1)}, bf16[3,192,128]{2,1,0:T(8,128)(2,1)S(1)}) fusion(bf16[16,192,128]{2,1,0:T(8,128)(2,1)} %get-tuple-element.17), kind=kLoop, calls=%fused_computation.28 | loop fusion | bytes 589824 | tf_op jit(solution)/shard_map/slice | solution.py:182
  64.5 3.5 %collective-permute-start.4 = (bf16[3,192,128]{2,1,0:T(8,128)(2,1)S(1)}, bf16[3,192,128]{2,1,0:T(8,128)(2,1)S(1)}, u32[]{:S(2)}, u32[]{:S(2)}) collective-permute-start(bf16[3,192,128]{2,1,0:T(8,128)(2,1)S(1)} %get-tuple-element.31), channel_id=1, source_target_pairs={{0,8},{8,16},{16,24},{1,9},{9,17},{17,25},{2,10},{10,18},{18,26},{... | collective-permute-start | bytes 442376 | tf_op jit(solution)/shard_map/ppermute | solution.py:182
  68.0 1.3 %collective-permute-start.5 = (bf16[3,192,128]{2,1,0:T(8,128)(2,1)S(1)}, bf16[3,192,128]{2,1,0:T(8,128)(2,1)S(1)}, u32[]{:S(2)}, u32[]{:S(2)}) collective-permute-start(bf16[3,192,128]{2,1,0:T(8,128)(2,1)S(1)} %get-tuple-element.30), channel_id=1, source_target_pairs={{8,0},{16,8},{24,16},{9,1},{17,9},{25,17},{10,2},{18,10},{26,18},{... | collective-permute-start | bytes 442376 | tf_op jit(solution)/shard_map/ppermute | solution.py:182
  69.3 2.8 %collective-permute-done.4 = bf16[3,192,128]{2,1,0:T(8,128)(2,1)S(1)} collective-permute-done((bf16[3,192,128]{2,1,0:T(8,128)(2,1)S(1)}, bf16[3,192,128]{2,1,0:T(8,128)(2,1)S(1)}, u32[]{:S(2)}, u32[]{:S(2)}) %collective-permute-start.4) | collective-permute-done | bytes 147488 | tf_op jit(solution)/shard_map/ppermute | solution.py:182
  72.2 0.1 constant_dynamic-update-slice_fusion.1
  72.3 4.0 %collective-permute-done.5 = bf16[3,192,128]{2,1,0:T(8,128)(2,1)S(1)} collective-permute-done((bf16[3,192,128]{2,1,0:T(8,128)(2,1)S(1)}, bf16[3,192,128]{2,1,0:T(8,128)(2,1)S(1)}, u32[]{:S(2)}, u32[]{:S(2)}) %collective-permute-start.5) | collective-permute-done | bytes 147488 | tf_op jit(solution)/shard_map/ppermute | solution.py:182
  76.3 0.5 slice_bitcast_fusion.1
  76.8 0.5 copy-done.1
  77.3 0.5 copy.41
  77.8 1.4 %collective-permute-start.6 = (bf16[3,22,192]{2,1,0:T(8,128)(2,1)S(1)}, bf16[3,22,192]{2,1,0:T(8,128)(2,1)S(1)}, u32[]{:S(2)}, u32[]{:S(2)}) collective-permute-start(bf16[3,22,192]{2,1,0:T(8,128)(2,1)S(1)} %copy.41), channel_id=1, source_target_pairs={{1,0},{2,1},{3,2},{4,3},{5,4},{6,5},{7,6},{0,7},{9,8},{10,9},{11,1... | collective-permute-start | bytes 76040 | tf_op jit(solution)/shard_map/ppermute | solution.py:185
  79.3 0.5 copy.43
  79.8 0.2 collective-permute-start.7
  80.0 0.8 copy.46
  80.8 0.1 collective-permute-done.6
  80.9 0.6 copy.42
  81.5 2.8 %collective-permute-done.7 = bf16[3,22,192]{2,1,0:T(8,128)(2,1)S(1)} collective-permute-done((bf16[3,22,192]{2,1,0:T(8,128)(2,1)S(1)}, bf16[3,22,192]{2,1,0:T(8,128)(2,1)S(1)}, u32[]{:S(2)}, u32[]{:S(2)}) %collective-permute-start.7) | collective-permute-done | bytes 25376 | tf_op jit(solution)/shard_map/ppermute | solution.py:186
  84.3 0.6 copy.44
  84.9 1.6 %pad_maximum_fusion.2.h_ref = bf16[22,192,128]{2,1,0:T(8,128)(2,1)} fusion(bf16[22,192,3]{2,1,0:T(8,128)(2,1)S(1)} %bitcast.29, bf16[22,192,3]{2,1,0:T(8,128)(2,1)S(1)} %bitcast.27, bf16[128]{0:T(256)(128)(2,1)S(1)} %pad.25.clone), kind=kLoop, calls=%fused_computation.6 | loop fusion | flops 3244032 | bytes 1132288 | tf_op jit(solution)/shard_map/concatenate | solution.py:187
  86.5 10.5 %shard_map.116 = bf16[16,192,128]{2,1,0:T(8,128)(2,1)} custom-call(bf16[22,192,128]{2,1,0:T(8,128)(2,1)} %copy-done.1, bf16[22,192,128]{2,1,0:T(8,128)(2,1)} %pad_maximum_fusion.2.h_ref, f32[192,128]{1,0:T(8,128)} %pad_convert_fusion.k_ref, f32[16,192,128]{2,1,0:T(8,128)} %get-tuple-element.18.fb_ref), custom_call_target="tpu_custom_call" | custom-call | flops 1000000000 | bytes 8388608 | tf_op jit(solution)/shard_map/pallas_call | solution.py:23
  97.0 2.5 %copy.45 = bf16[192,16,128]{2,1,0:T(8,128)(2,1)} copy(bf16[192,16,128]{2,0,1:T(8,128)(2,1)} %bitcast.31) | data formatting | bytes 1572864
  (30 shorter events, 0.2 us)
Async XLA Ops:
  7.2 1.9 %copy-start.3 = (bf16[192,16,128]{2,1,0:T(8,128)(2,1)S(1)}, bf16[192,16,128]{2,1,0:T(8,128)(2,1)}, u32[]{:S(2)}) copy-start(bf16[192,16,128]{2,1,0:T(8,128)(2,1)} %param.10) | copy-start | bytes 2359300
  7.2 43.2 %all-gather.3.cloned.1.call-start = ((), (), s32[]{:S(2)}) async-start(), calls=%async_computation | async-start | bytes 3244032 | tf_op jit(solution)/shard_map/all_gather | solution.py:218
  9.1 6.5 %slice-start = ((s32[512,4]{0,1:T(4,128)}), s32[512,1]{0,1:T(1,128)S(1)}, s32[]{:S(2)}) async-start(s32[512,4]{0,1:T(4,128)} %param.13), calls=%async_computation.1 | async-start | bytes 4096 | tf_op jit(solution)/shard_map/slice | solution.py:221
  9.1 6.7 %copy-start.7 = (bf16[192,7,7]{0,2,1:T(8,128)(2,1)S(1)}, bf16[192,7,7]{0,2,1:T(8,128)(2,1)}, u32[]{:S(2)}) copy-start(bf16[192,7,7]{0,2,1:T(8,128)(2,1)} %param.11) | copy-start | bytes 56452
  9.4 8.1 %collective-permute-start = (bf16[3,192,128]{2,1,0:T(8,128)(2,1)S(1)}, bf16[3,192,128]{2,1,0:T(8,128)(2,1)S(1)}, u32[]{:S(2)}, u32[]{:S(2)}) collective-permute-start(bf16[3,192,128]{2,1,0:T(8,128)(2,1)S(1)} %get-tuple-element.32), channel_id=1, source_target_pairs={{0,8},{8,16},{16,24},{1,9},{9,17},{17,25},{2,10},{10,18},{18,26},{... | collective-permute-start | bytes 442376 | tf_op jit(solution)/shard_map/ppermute | solution.py:182
  14.3 7.2 %collective-permute-start.1 = (bf16[3,192,128]{2,1,0:T(8,128)(2,1)S(1)}, bf16[3,192,128]{2,1,0:T(8,128)(2,1)S(1)}, u32[]{:S(2)}, u32[]{:S(2)}) collective-permute-start(bf16[3,192,128]{2,1,0:T(8,128)(2,1)S(1)} %get-tuple-element.33), channel_id=1, source_target_pairs={{8,0},{16,8},{24,16},{9,1},{17,9},{25,17},{10,2},{18,10},{26,18},{... | collective-permute-start | bytes 442376 | tf_op jit(solution)/shard_map/ppermute | solution.py:182
  21.7 1.0 copy-start
  22.7 2.6 %copy-start.8 = (s32[512,1]{0,1:T(1,128)S(1)}, s32[512,1]{0,1:T(1,128)}, u32[]{:S(2)}) copy-start(s32[512,1]{0,1:T(1,128)} %param.15) | copy-start | bytes 6148
  22.7 3.5 %copy-start.6 = (bf16[512,137]{0,1:T(8,128)(2,1)S(1)}, bf16[512,137]{0,1:T(8,128)(2,1)}, u32[]{:S(2)}) copy-start(bf16[512,137]{0,1:T(8,128)(2,1)} %param.16) | copy-start | bytes 420868
  23.2 3.8 %copy-start.9 = (bf16[512,4]{0,1:T(4,128)(2,1)S(1)}, bf16[512,4]{0,1:T(4,128)(2,1)}, u32[]{:S(2)}) copy-start(bf16[512,4]{0,1:T(4,128)(2,1)} %param.14) | copy-start | bytes 12292
  23.2 4.6 %copy-start.4 = (bf16[192,192]{1,0:T(8,128)(2,1)S(1)}, bf16[192,192]{1,0:T(8,128)(2,1)}, u32[]{:S(2)}) copy-start(bf16[192,192]{1,0:T(8,128)(2,1)} %refs_6_.1) | copy-start | bytes 221188
  23.2 9.4 %collective-permute-start.2 = (bf16[3,22,192]{2,1,0:T(8,128)(2,1)S(1)}, bf16[3,22,192]{2,1,0:T(8,128)(2,1)S(1)}, u32[]{:S(2)}, u32[]{:S(2)}) collective-permute-start(bf16[3,22,192]{2,1,0:T(8,128)(2,1)S(1)} %copy.31), channel_id=1, source_target_pairs={{1,0},{2,1},{3,2},{4,3},{5,4},{6,5},{7,6},{0,7},{9,8},{10,9},{11,1... | collective-permute-start | bytes 76040 | tf_op jit(solution)/shard_map/ppermute | solution.py:185
  24.6 8.7 %collective-permute-start.3 = (bf16[3,22,192]{2,1,0:T(8,128)(2,1)S(1)}, bf16[3,22,192]{2,1,0:T(8,128)(2,1)S(1)}, u32[]{:S(2)}, u32[]{:S(2)}) collective-permute-start(bf16[3,22,192]{2,1,0:T(8,128)(2,1)S(1)} %copy.33), channel_id=1, source_target_pairs={{0,1},{1,2},{2,3},{3,4},{4,5},{5,6},{6,7},{7,0},{8,9},{9,10},{10,1... | collective-permute-start | bytes 76040 | tf_op jit(solution)/shard_map/ppermute | solution.py:186
  63.4 8.7 %copy-start.2 = (bf16[16,192,128]{2,1,0:T(8,128)(2,1)S(1)}, bf16[16,192,128]{2,1,0:T(8,128)(2,1)}, u32[]{:S(2)}) copy-start(bf16[16,192,128]{2,1,0:T(8,128)(2,1)} %get-tuple-element.17) | copy-start | bytes 2359300
  64.5 7.6 %collective-permute-start.4 = (bf16[3,192,128]{2,1,0:T(8,128)(2,1)S(1)}, bf16[3,192,128]{2,1,0:T(8,128)(2,1)S(1)}, u32[]{:S(2)}, u32[]{:S(2)}) collective-permute-start(bf16[3,192,128]{2,1,0:T(8,128)(2,1)S(1)} %get-tuple-element.31), channel_id=1, source_target_pairs={{0,8},{8,16},{16,24},{1,9},{9,17},{17,25},{2,10},{10,18},{18,26},{... | collective-permute-start | bytes 442376 | tf_op jit(solution)/shard_map/ppermute | solution.py:182
  68.0 8.2 %collective-permute-start.5 = (bf16[3,192,128]{2,1,0:T(8,128)(2,1)S(1)}, bf16[3,192,128]{2,1,0:T(8,128)(2,1)S(1)}, u32[]{:S(2)}, u32[]{:S(2)}) collective-permute-start(bf16[3,192,128]{2,1,0:T(8,128)(2,1)S(1)} %get-tuple-element.30), channel_id=1, source_target_pairs={{8,0},{16,8},{24,16},{9,1},{17,9},{25,17},{10,2},{18,10},{26,18},{... | collective-permute-start | bytes 442376 | tf_op jit(solution)/shard_map/ppermute | solution.py:182
  76.3 1.0 copy-start.1
  77.3 2.8 %copy-start.5 = (bf16[512,137]{1,0:T(8,128)(2,1)S(1)}, bf16[512,137]{1,0:T(8,128)(2,1)}, u32[]{:S(2)}) copy-start(bf16[512,137]{1,0:T(8,128)(2,1)} %get-tuple-element.25) | copy-start | bytes 420868
  77.8 3.1 %collective-permute-start.6 = (bf16[3,22,192]{2,1,0:T(8,128)(2,1)S(1)}, bf16[3,22,192]{2,1,0:T(8,128)(2,1)S(1)}, u32[]{:S(2)}, u32[]{:S(2)}) collective-permute-start(bf16[3,22,192]{2,1,0:T(8,128)(2,1)S(1)} %copy.41), channel_id=1, source_target_pairs={{1,0},{2,1},{3,2},{4,3},{5,4},{6,5},{7,6},{0,7},{9,8},{10,9},{11,1... | collective-permute-start | bytes 76040 | tf_op jit(solution)/shard_map/ppermute | solution.py:185
  79.8 4.5 %collective-permute-start.7 = (bf16[3,22,192]{2,1,0:T(8,128)(2,1)S(1)}, bf16[3,22,192]{2,1,0:T(8,128)(2,1)S(1)}, u32[]{:S(2)}, u32[]{:S(2)}) collective-permute-start(bf16[3,22,192]{2,1,0:T(8,128)(2,1)S(1)} %copy.43), channel_id=1, source_target_pairs={{0,1},{1,2},{2,3},{3,4},{4,5},{5,6},{6,7},{7,0},{8,9},{9,10},{10,1... | collective-permute-start | bytes 76040 | tf_op jit(solution)/shard_map/ppermute | solution.py:186
Sparse Core Ops, SparseCore 0:
  9.9 34.4 all-gather.2
where the time goes:
time: 107 us; the launch traced here: 106 us
  Pallas kernels  42.4 us (40%)
  local copies, waits for them, and re-layouts  14.7 us (14%)
  waiting for transfers between devices  14.3 us (13%)
  between operations  14.3 us (13%)
  starting transfers between devices  13.6 us (13%)
  other arithmetic  7.01 us (7%)
    pallas_call x4, Pallas kernels, call(): pl.pallas_call(kernel, out_shape=out_shape, in_specs=[VM] * len(args), ou...  42.4 us
    ppermute x2, starting transfers between devices, halo(): lax.ppermute(x[-3:], 'lat', up)  8.47 us
    ppermute x2, waiting for transfers between devices, halo(): lax.ppermute(x[:3], 'lat', down)  8.11 us
    unnamed x30, local copies, waits for them, and re-layouts  8.05 us
    concatenate x2, other arithmetic, halo(): jnp.concatenate([head, jnp.zeros((rows, channels, breadth - 6), x.dtype),...  3.36 us
    ppermute x2, waiting for transfers between devices, halo(): lax.ppermute(x[-3:], 'lat', up)  3.24 us
    ppermute x2, waiting for transfers between devices, halo(): lax.ppermute(x[:, :, -3:].transpose(2, 0, 1), 'lon', right)  2.85 us
    ppermute x2, starting transfers between devices, halo(): lax.ppermute(x[:3], 'lat', down)  2.58 us
  transfers between devices with their start and end apart: 9, of which 6 were waited for; matrix products, arithmetic and copies ran while one was open for 11% of the time, Pallas kernels for 18%

commit v1 on v0

v1 whole, which is shorter than its diff:
```python
import jax
import jax.numpy as jnp
from jax import lax
from jax.experimental import pallas as pl
from jax.experimental.pallas import tpu as pltpu
from jax.sharding import PartitionSpec as P

CAP = 64
F32 = jnp.float32
BF = jnp.bfloat16
VM = pl.BlockSpec(memory_space=pltpu.VMEM)


def nn(a, b):
    return jnp.dot(a, b, preferred_element_type=F32)


def nt(a, b):
    return lax.dot_general(a, b, (((1,), (1,)), ((), ())), preferred_element_type=F32)


def conv_group(x_ref, h_ref, k_ref, base, flip):
    rows = x_ref.shape[0]
    breadth = x_ref.shape[2]
    height = rows - 6
    lane = lax.broadcasted_iota(jnp.int32, (16, breadth), 1)
    taps = k_ref[pl.ds(base, 16), :]
    acc = [None] * height
    for col in range(7):
        shift = col - 3
        weights = []
        for row in range(7):
            t = (6 - row) * 7 + 6 - col if flip else row * 7 + col
            weights.append(jnp.broadcast_to(taps[:, t : t + 1], (16, breadth)))
        for r in range(rows):
            v = x_ref[r, pl.ds(base, 16), :].astype(F32)
            if shift:
                edge = h_ref[r, pl.ds(base, 16), :].astype(F32)
                mask = lane < shift if shift > 0 else lane >= breadth + shift
                v = pltpu.roll(jnp.where(mask, edge, v), (-shift) % breadth, 1)
            for row in range(7):
                i = r - row
                if 0 <= i < height:
                    term = weights[row] * v
                    acc[i] = term if acc[i] is None else acc[i] + term
    return acc


def prepare(owner_row, owner_col, row0, col0, w_ref, obs_ref, wt_ref, p_ref, pt_ref, obs_slot):
    height, obs, breadth = wt_ref.shape
    slots = p_ref.shape[0]
    n = slots // CAP
    lane = lax.broadcasted_iota(jnp.int32, (obs, breadth), 1)
    c0 = jnp.broadcast_to(col0[...], (obs, breadth))
    r0 = jnp.broadcast_to(row0[...], (obs, breadth))
    w = w_ref[...].astype(F32)
    zero = jnp.zeros((obs, breadth), F32)
    first = lane == c0
    second = lane == c0 + 1
    top = jnp.where(first, w[:, 0:1], jnp.where(second, w[:, 1:2], zero))
    bottom = jnp.where(first, w[:, 2:3], jnp.where(second, w[:, 3:4], zero))
    for r in range(height):
        wt_ref[r] = jnp.where(r0 == r, top, jnp.where(r0 == r - 1, bottom, zero)).astype(BF)
    si = lax.broadcasted_iota(jnp.int32, (obs, obs), 0)
    sj = lax.broadcasted_iota(jnp.int32, (obs, obs), 1)
    ones_u = jnp.where(si < sj, 1.0, 0.0).astype(BF)
    ones_l = jnp.where(sj < si, 1.0, 0.0).astype(BF)
    own = owner_row[...]
    hot = jnp.where(lax.broadcasted_iota(jnp.int32, (n, obs), 0) == own, 1.0, 0.0)
    within = jnp.sum(nn(hot.astype(BF), ones_u) * hot, axis=0, keepdims=True)
    slot_row = own * CAP + within.astype(jnp.int32)
    place = lax.broadcasted_iota(jnp.int32, (slots, obs), 0) == slot_row
    p = jnp.where(place, 1.0, 0.0).astype(BF)
    p_ref[...] = p
    own = owner_col[...]
    hot = jnp.where(lax.broadcasted_iota(jnp.int32, (obs, 128), 1) == own, 1.0, 0.0)
    within = jnp.sum(nn(ones_l, hot.astype(BF)) * hot, axis=1, keepdims=True)
    slot_col = own * CAP + within.astype(jnp.int32)
    place = lax.broadcasted_iota(jnp.int32, (obs, slots), 1) == slot_col
    pt_ref[...] = jnp.where(place, 1.0, 0.0).astype(BF)
    obs_slot[...] = nn(p, obs_ref[...]).astype(BF)


def remote(src, dst, send, recv, device):
    return pltpu.make_async_remote_copy(
        src_ref=src,
        dst_ref=dst,
        send_sem=send,
        recv_sem=recv,
        device_id=device,
        device_id_type=pl.DeviceIdType.MESH,
    )


def selector(breadth):
    s = lax.broadcasted_iota(jnp.int32, (8, breadth), 0)
    lane = lax.broadcasted_iota(jnp.int32, (8, breadth), 1)
    near = (s < 3) & (lane == s)
    far = (s > 4) & (lane == s + (breadth - 8))
    return jnp.where(near | far, 1.0, 0.0).astype(BF)


def copies(src, off, x, edge, right_in, left_in, send, recv, lats, lons):
    height = edge.shape[0]
    lat, lon = lax.axis_index("lat"), lax.axis_index("lon")
    left, right = lax.rem(lon + lons - 1, lons), lax.rem(lon + 1, lons)
    low, high, mid = pl.ds(0, 3), pl.ds(height + 3, 3), pl.ds(3, height)
    end = pl.ds(height - 3, 3)

    def make(i, a, b, device):
        return remote(a, b, send.at[i], recv.at[i], device)

    side = [
        make(2, edge, right_in.at[mid], {"lat": lat, "lon": left}),
        make(3, edge, left_in.at[mid], {"lat": lat, "lon": right}),
    ]
    u, d = lax.max(lat - 1, 0), lax.min(lat + 1, lats - 1)
    up = [
        make(0, src.at[pl.ds(off, 3)], x.at[high], {"lat": u, "lon": lon}),
        make(4, edge.at[low], right_in.at[high], {"lat": u, "lon": left}),
        make(5, edge.at[low], left_in.at[high], {"lat": u, "lon": right}),
    ]
    down = [
        make(1, src.at[pl.ds(off + height - 3, 3)], x.at[low], {"lat": d, "lon": lon}),
        make(6, edge.at[end], right_in.at[low], {"lat": d, "lon": left}),
        make(7, edge.at[end], left_in.at[low], {"lat": d, "lon": right}),
    ]
    return lat > 0, lat < lats - 1, up, down, side


def start_exchange(src, off, x, edge, right_in, left_in, send, recv, lats, lons):
    height = edge.shape[0]
    pick = selector(x.shape[2])
    has_up, has_down, up, down, side = copies(
        src, off, x, edge, right_in, left_in, send, recv, lats, lons
    )
    pl.when(has_up)(lambda: up[0].start())
    pl.when(has_down)(lambda: down[0].start())

    def row(r, carry):
        edge[r] = nt(pick, src[off + r]).astype(BF)
        return carry

    lax.fori_loop(0, height, row, 0, unroll=4)
    for copy in side:
        copy.start()

    @pl.when(has_up)
    def _():
        up[1].start()
        up[2].start()

    @pl.when(has_down)
    def _():
        down[1].start()
        down[2].start()

    for missing, at in ((lat_first(has_up), 0), (lat_first(has_down), height + 3)):

        @pl.when(missing)
        def _():
            for ref in (x, right_in, left_in):
                ref[at : at + 3] = jnp.zeros((3,) + ref.shape[1:], BF)


def lat_first(has):
    return jnp.logical_not(has)


def end_exchange(src, off, x, edge, right_in, left_in, halo, send, recv, lats, lons):
    has_up, has_down, up, down, side = copies(
        src, off, x, edge, right_in, left_in, send, recv, lats, lons
    )

    @pl.when(has_up)
    def _():
        for copy in down:
            copy.wait_recv()
        for copy in up:
            copy.wait_send()

    @pl.when(has_down)
    def _():
        for copy in up:
            copy.wait_recv()
        for copy in down:
            copy.wait_send()

    for copy in side:
        copy.wait()
    pick = selector(x.shape[2])
    near = lax.broadcasted_iota(jnp.int32, (8, x.shape[1]), 0) < 4

    def row(r, carry):
        both = jnp.where(near, right_in[r].astype(F32), left_in[r].astype(F32))
        halo[r] = nn(both.T.astype(BF), pick).astype(BF)
        return carry

    lax.fori_loop(0, x.shape[0], row, 0, unroll=2)


def kernel(
    lats,
    lons,
    state,
    op_ref,
    owner_row,
    owner_col,
    row0,
    col0,
    w_ref,
    obs_ref,
    k_ref,
    pwt_ref,
    pw_ref,
    out_ref,
    dep_ref,
    x1,
    x2,
    halo,
    edge,
    right_in,
    left_in,
    ops,
    wt,
    p_mat,
    pt_mat,
    obs_slot,
    mixed,
    grid_f,
    total,
    prof,
    adj,
    mis,
    send,
    recv,
    op_send,
    op_recv,
):
    height, channels, breadth = state.shape
    levels = obs_ref.shape[1]
    lat, lon = lax.axis_index("lat"), lax.axis_index("lon")
    partner = lon + 1 - 2 * lax.rem(lon, 2)
    other = lax.rem(lon + lons - 1 + 2 * lax.rem(lon, 2), lons)
    half = lons // 2
    peers = [lax.rem(lon + 2 * j, lons) for j in range(1, half)]
    barrier = pltpu.get_barrier_semaphore()

    def greet(a, b):
        pl.semaphore_signal(
            barrier,
            inc=1,
            device_id={"lat": a, "lon": b},
            device_id_type=pl.DeviceIdType.MESH,
        )

    for b in [partner, other] + peers:
        greet(lat, b)

    @pl.when(lat > 0)
    def _():
        for b in (partner, lon, other):
            greet(lat - 1, b)

    @pl.when(lat < lats - 1)
    def _():
        for b in (partner, lon, other):
            greet(lat + 1, b)

    sides = lax.min(lat, 1) + lax.min(lats - 1 - lat, 1)
    pl.semaphore_wait(barrier, half + 1 + 3 * sides)

    def wires(k):
        return edge.at[k], right_in.at[k], left_in.at[k]

    start_exchange(state, 0, x1, *wires(0), send.at[0], recv.at[0], lats, lons)
    sends = [
        remote(op_ref, ops.at[lon], op_send.at[j], op_recv.at[lon], {"lat": lat, "lon": b})
        for j, b in enumerate([partner] + peers)
    ]
    for copy in sends:
        copy.start()
    x1[3 : 3 + height] = state[...]
    ops[lon] = op_ref[...]
    prepare(owner_row, owner_col, row0, col0, w_ref, obs_ref, wt, p_mat, pt_mat, obs_slot)
    end_exchange(state, 0, x1, *wires(0), halo, send.at[0], recv.at[0], lats, lons)

    def group(g, carry):
        base = pl.multiple_of(g * 16, 16)
        for i, v in enumerate(conv_group(x1, halo, k_ref, base, False)):
            mixed[i, pl.ds(base, 16), :] = v.astype(BF)
        return carry

    lax.fori_loop(0, channels // 16, group, 0)

    forwards = []
    for j, b in enumerate(peers):
        copy = remote(
            ops.at[b], ops.at[b], op_send.at[half + j], op_recv.at[b], {"lat": lat, "lon": partner}
        )
        copy.wait_recv()
        copy.start()
        forwards.append(copy)

    total[...] = jnp.zeros_like(total)
    a, c3 = 0.7978845608028654, 0.044715

    def ahead(q, carry):
        r = q * 2
        pre = nn(pwt_ref[...], jnp.concatenate([mixed[r], mixed[r + 1]], axis=1))
        square = pre * pre
        t = jnp.tanh(a * (pre + c3 * (square * pre)))
        gate = 0.5 * (1.0 + t)
        slope = gate + (0.5 * pre) * (1.0 - t * t) * (a * (1.0 + (3.0 * c3) * square))
        grid_f[r] = slope[:, :breadth]
        grid_f[r + 1] = slope[:, breadth:]
        here = jnp.concatenate([state[r], state[r + 1]], axis=1).astype(F32)
        analysis = (here + pre * gate).astype(BF)
        total[...] += nt(jnp.concatenate([wt[r], wt[r + 1]], axis=1), analysis)
        return carry

    lax.fori_loop(0, height // 2, ahead, 0)
    prof[...] = nn(p_mat[...], total[...].astype(BF)).astype(BF)

    for j in range(half):
        b = lax.rem(partner + 2 * j, lons)
        remote(
            ops.at[b], ops.at[b], op_send.at[0], op_recv.at[b], {"lat": lat, "lon": partner}
        ).wait_recv()
    err_row = op_ref.shape[0] - 16

    def instrument(o, carry):
        at = pl.ds(pl.multiple_of(o * CAP, CAP), CAP)
        hw = ops[o, :channels, :]
        lw = ops[o, channels : channels + levels, :]
        err = ops[o, err_row : err_row + 1, :levels].astype(F32)
        squashed = jnp.tanh(nn(prof[at, :], hw))
        misfit = nt(squashed.astype(BF), lw) - obs_slot[at, :].astype(F32)
        mis[at, :] = misfit.astype(BF)
        back = nn((err * misfit).astype(BF), lw) * (1.0 - squashed * squashed)
        adj[at, :] = nt(back.astype(BF), hw).astype(BF)
        return carry

    lax.fori_loop(0, lons, instrument, 0, unroll=4)
    dep_ref[...] = nn(pt_mat[...], mis[...]).astype(BF)
    adj_t = nn(pt_mat[...], adj[...]).T.astype(BF)

    def behind(q, carry):
        r = q * 2
        fb = nn(adj_t, jnp.concatenate([wt[r], wt[r + 1]], axis=1))
        gate = (fb * jnp.concatenate([grid_f[r], grid_f[r + 1]], axis=1)).astype(BF)
        grid_f[r] = fb[:, :breadth]
        grid_f[r + 1] = fb[:, breadth:]
        mb = nn(pw_ref[...], gate).astype(BF)
        x2[r + 3] = mb[:, :breadth]
        x2[r + 4] = mb[:, breadth:]
        return carry

    lax.fori_loop(0, height // 2, behind, 0)
    for copy in sends + forwards:
        copy.wait_send()
    start_exchange(x2, 3, x2, *wires(1), send.at[1], recv.at[1], lats, lons)
    end_exchange(x2, 3, x2, *wires(1), halo, send.at[1], recv.at[1], lats, lons)

    def group_back(g, carry):
        base = pl.multiple_of(g * 16, 16)
        for i, v in enumerate(conv_group(x2, halo, k_ref, base, True)):
            out_ref[i, pl.ds(base, 16), :] = (v + grid_f[i, pl.ds(base, 16), :]).astype(BF)
        return carry

    lax.fori_loop(0, channels // 16, group_back, 0)


def body(
    state,
    depth_kernel,
    point_weight,
    column_index,
    column_weight,
    owner,
    observed,
    hidden_weight,
    level_weight,
    inverse_error,
):
    channels, height, breadth = state.shape
    obs, levels = observed.shape
    hid = hidden_weight.shape[2]
    lats, n = lax.axis_size("lat"), lax.axis_size("lon")
    slots = n * CAP
    fill = (-(channels + levels)) % 16
    pack = jnp.concatenate(
        [
            hidden_weight[0],
            jnp.pad(level_weight[0].T, ((0, fill), (0, 0))),
            jnp.pad(inverse_error, ((0, 15), (0, hid - levels))),
        ],
        axis=0,
    )
    taps = jnp.pad(depth_kernel.reshape(channels, 49).astype(F32), ((0, 0), (0, 79)))
    row0 = column_index[:, :1] // breadth
    col0 = column_index[:, :1] - row0 * breadth
    args = (
        state.transpose(1, 0, 2),
        pack,
        owner.reshape(1, obs),
        owner,
        row0,
        col0,
        column_weight,
        observed,
        taps,
        point_weight.T,
        point_weight,
    )
    rows = height + 6
    grid = (rows, channels, breadth)
    vm = pltpu.VMEM
    grad, departures = pl.pallas_call(
        lambda *refs: kernel(lats, n, *refs),
        out_shape=(
            jax.ShapeDtypeStruct((height, channels, breadth), BF),
            jax.ShapeDtypeStruct((obs, levels), BF),
        ),
        in_specs=[VM] * len(args),
        out_specs=(VM, VM),
        scratch_shapes=[
            vm(grid, BF),
            vm(grid, BF),
            vm(grid, BF),
            vm((2, height, 8, channels), BF),
            vm((2, rows, 8, channels), BF),
            vm((2, rows, 8, channels), BF),
            vm((n,) + pack.shape, BF),
            vm((height, obs, breadth), BF),
            vm((slots, obs), BF),
            vm((obs, slots), BF),
            vm((slots, levels), BF),
            vm((height, channels, breadth), BF),
            vm((height, channels, breadth), F32),
            vm((obs, channels), F32),
            vm((slots, channels), BF),
            vm((slots, channels), BF),
            vm((slots, levels), BF),
            pltpu.SemaphoreType.DMA((2, 8)),
            pltpu.SemaphoreType.DMA((2, 8)),
            pltpu.SemaphoreType.DMA((n,)),
            pltpu.SemaphoreType.DMA((n,)),
        ],
        compiler_params=pltpu.CompilerParams(
            vmem_limit_bytes=56 << 20, collective_id=0, has_side_effects=True
        ),
    )(*args)
    return (grad.transpose(1, 0, 2), departures)


def solution(mesh):
    in_specs = (
        P(None, "lat", "lon"),
        P(),
        P(),
        P(("lat", "lon"), None),
        P(("lat", "lon"), None),
        P(("lat", "lon"), None),
        P(("lat", "lon"), None),
        P("lon", None, None),
        P("lon", None, None),
        P("lon", None),
    )
    out_specs = (P(None, "lat", "lon"), P(("lat", "lon"), None))
    return jax.shard_map(body, mesh=mesh, in_specs=in_specs, out_specs=out_specs, check_vma=False)
```

time: 107 us -> 67.7 us (0.63)
  waiting for transfers between devices: 14.3 us -> 0 us
  between operations: 14.3 us -> 0.68 us
  starting transfers between devices: 13.6 us -> 0 us
  Pallas kernels: 42.4 us -> 53.7 us
  local copies, waits for them, and re-layouts: 14.7 us -> 9.64 us
  other arithmetic: 7.01 us -> 2.39 us
    ppermute x8 -> x0, waiting for transfers between devices: 14.3 us -> none  [the longest x2 8.11 us: halo(): lax.ppermute(x[:3], 'lat', down)]
    ppermute x8 -> x0, starting transfers between devices: 13.6 us -> none  [the longest x2 8.47 us: halo(): lax.ppermute(x[-3:], 'lat', up)]
    pallas_call x4 -> x1, Pallas kernels: 42.4 us -> 53.7 us  [body(): pl.pallas_call(lambda *refs: kernel(lats, n, *refs), out_shape=(jax.Shape...]
    concatenate x3 -> x0, other arithmetic: 3.49 us -> none  [the longest x2 3.36 us: halo(): jnp.concatenate([head, jnp.zeros((rows, channels, breadth - 6), x.dtype),...]
    transpose x6 -> x0, local copies, waits for them, and re-layouts: 3.11 us -> none  [the longest x4 2.04 us: halo(): x[:, :, :3].transpose(2, 0, 1)]
    ppermute x4 -> x0, local copies, waits for them, and re-layouts: 2.23 us -> none  [the longest x2 1.11 us: halo(): lax.ppermute(x[:, :, -3:].transpose(2, 0, 1), 'lon', right)]
    slice x2 -> x0, local copies, waits for them, and re-layouts: 1.1 us -> none  [the longest x1 1.07 us: halo(): x[:3]]
    concatenate x1, other arithmetic: 1.85 us -> 0.78 us  [body(): jnp.concatenate([hidden_weight[0], jnp.pad(level_weight[0].T, ((0, fill),...]
  transfers between devices with their start and end apart: 9 -> 0, of which waited for: 6 -> 0; matrix products, arithmetic and copies ran while one was open for 11% -> 0% of each run, Pallas kernels for 18% -> 0%
where the time goes in v1:
time: 67.7 us; the launch traced here: 66.4 us
  Pallas kernels  53.7 us (79%)
  local copies, waits for them, and re-layouts  9.64 us (14%)
  other arithmetic  2.39 us (4%)
  between operations  0.68 us (1%)
    pallas_call x1, Pallas kernels, body(): pl.pallas_call(lambda *refs: kernel(lats, n, *refs), out_shape=(jax.Shape...  53.7 us
    unnamed x26, local copies, waits for them, and re-layouts  8.75 us

profile of v1, /device:TPU:0, one launch (start us, length us, event | category | flops | bytes accessed | tf_op | source)
XLA Modules:
  0.0 66.4 jit_solution(5563565922495517812)
XLA Ops:
  0.6 0.8 %convert_element_type.10 = bf16[192,49]{0,1:T(8,128)(2,1)S(1)} reshape(bf16[192,7,7]{0,2,1:T(8,128)(2,1)} %param.11) | data formatting | bytes 37632 | tf_op jit(solution)/shard_map/convert_element_type | solution.py:400
  1.4 0.0 copy-start.1
  1.4 0.1 copy.23
  1.5 0.7 pad_convert_fusion.refs_8_
  2.2 0.1 copy-done.1
  2.3 0.0 copy-start.7
  2.3 0.8 %copy.24 = bf16[192,192]{0,1:T(8,128)(2,1)} copy(bf16[192,192]{1,0:T(8,128)(2,1)S(1)} %copy-done.1) | data formatting | bytes 147456 | tf_op args[2]
  3.1 0.0 copy-done.7
  3.1 0.0 slice-start
  3.1 0.8 %copy.26.refs_6_ = bf16[512,4]{1,0:T(8,128)(2,1)} copy(bf16[512,4]{0,1:T(4,128)(2,1)S(1)} %copy-done.7) | data formatting | bytes 8192 | tf_op args[4]
  3.9 0.0 slice-done
  3.9 0.0 copy-start.4
  3.9 0.1 copy.30
  4.0 0.8 %copy-done.4 = bf16[512,137]{0,1:T(8,128)(2,1)S(1)} copy-done((bf16[512,137]{0,1:T(8,128)(2,1)S(1)}, bf16[512,137]{0,1:T(8,128)(2,1)}, u32[]{:S(2)}) %copy-start.4) | copy-done | bytes 140312
  4.8 0.0 copy-start.6
  4.8 0.9 %copy.27.refs_7_ = bf16[512,137]{1,0:T(8,128)(2,1)} copy(bf16[512,137]{0,1:T(8,128)(2,1)S(1)} %copy-done.4) | data formatting | bytes 280576 | tf_op args[6]
  5.6 0.0 copy-done.6
  5.6 0.0 copy-start.3
  5.6 0.0 copy-start.5
  5.6 0.0 copy-start.8
  5.7 0.9 %copy.25.refs_3_ = s32[512,1]{1,0:T(8,128)} copy(s32[512,1]{0,1:T(1,128)S(1)} %copy-done.6) | data formatting | bytes 4096 | tf_op args[5]
  6.5 0.0 copy-start
  6.5 1.0 %multiply_subtract_fusion = (s32[512,1]{1,0:T(8,128)}, s32[512,1]{1,0:T(8,128)}) fusion(s32[512,1]{1,0:T(8,128)S(1)} %copy.30), kind=kLoop, calls=%fused_computation.14 | loop fusion | flops 8704 | bytes 6144 | tf_op jit(solution)/shard_map/sub | solution.py:402
  7.5 0.0 copy-done.3
  7.5 0.0 copy-done.5
  7.5 0.0 copy-done.8
  7.5 0.8 %fusion.4.refs_1_ = bf16[352,512]{1,0:T(8,128)(2,1)} fusion(bf16[1,137]{1,0:T(2,128)(2,1)S(1)} %copy-done.8, bf16[137,512]{1,0:T(8,128)(2,1)S(1)} %bitcast.16, bf16[192,512]{1,0:T(8,128)(2,1)S(1)} %bitcast.15), kind=kLoop, calls=%fused_computation.12 | loop fusion | flops 2162688 | bytes 697618 | tf_op jit(solution)/shard_map/concatenate | solution.py:392
  8.3 0.0 copy-done
  8.3 1.1 %copy.32 = bf16[192,16,128]{2,0,1:T(8,128)(2,1)} copy(bf16[192,16,128]{2,1,0:T(8,128)(2,1)S(1)} %copy-done) | data formatting | bytes 1572864 | tf_op args[0]
  9.4 53.7 %shard_map.113 = (bf16[16,192,128]{2,1,0:T(8,128)(2,1)}, bf16[512,137]{1,0:T(8,128)(2,1)}) custom-call(bf16[16,192,128]{2,1,0:T(8,128)(2,1)} %bitcast.12, bf16[352,512]{1,0:T(8,128)(2,1)} %fusion.4.refs_1_, s32[1,512]{1,0:T(1,128)} %bitcast.17, s32[512,1]{1,0:T(8,128)} %copy.25.refs_3_, s32[512,1]{1,0:T(8,128)} %get-tuple-element.11.refs_4_, ...), custom_call_target="tpu_custom_call" | custom-call | tf_op jit(solution)/shard_map/pallas_call | solution.py:419
  63.1 0.0 copy-start.2
  63.1 2.6 %copy.28 = bf16[192,16,128]{2,1,0:T(8,128)(2,1)} copy(bf16[192,16,128]{2,0,1:T(8,128)(2,1)} %bitcast.13) | data formatting | bytes 1572864
  65.7 0.0 copy-done.2
  65.7 0.8 %copy.29 = bf16[512,137]{0,1:T(8,128)(2,1)} copy(bf16[512,137]{1,0:T(8,128)(2,1)S(1)} %copy-done.2) | data formatting | bytes 280576
Async XLA Ops:
  1.4 0.9 %copy-start.1 = (bf16[192,192]{1,0:T(8,128)(2,1)S(1)}, bf16[192,192]{1,0:T(8,128)(2,1)}, u32[]{:S(2)}) copy-start(bf16[192,192]{1,0:T(8,128)(2,1)} %refs_10_.1) | copy-start | bytes 221188
  2.3 0.8 %copy-start.7 = (bf16[512,4]{0,1:T(4,128)(2,1)S(1)}, bf16[512,4]{0,1:T(4,128)(2,1)}, u32[]{:S(2)}) copy-start(bf16[512,4]{0,1:T(4,128)(2,1)} %param.14) | copy-start | bytes 12292
  3.1 0.8 %slice-start = ((s32[512,4]{0,1:T(4,128)}), s32[512,1]{0,1:T(1,128)S(1)}, s32[]{:S(2)}) async-start(s32[512,4]{0,1:T(4,128)} %param.13), calls=%async_computation | async-start | bytes 4096 | tf_op jit(solution)/shard_map/slice | solution.py:401
  3.9 0.9 %copy-start.4 = (bf16[512,137]{0,1:T(8,128)(2,1)S(1)}, bf16[512,137]{0,1:T(8,128)(2,1)}, u32[]{:S(2)}) copy-start(bf16[512,137]{0,1:T(8,128)(2,1)} %param.16) | copy-start | bytes 420868
  4.8 0.9 %copy-start.6 = (s32[512,1]{0,1:T(1,128)S(1)}, s32[512,1]{0,1:T(1,128)}, u32[]{:S(2)}) copy-start(s32[512,1]{0,1:T(1,128)} %param.15) | copy-start | bytes 6148
  5.6 1.8 %copy-start.3 = (bf16[1,192,512]{2,1,0:T(8,128)(2,1)S(1)}, bf16[1,192,512]{2,1,0:T(8,128)(2,1)}, u32[]{:S(2)}) copy-start(bf16[1,192,512]{2,1,0:T(8,128)(2,1)} %param.17) | copy-start | bytes 589828
  5.6 1.8 %copy-start.5 = (bf16[1,512,137]{1,2,0:T(8,128)(2,1)S(1)}, bf16[1,512,137]{1,2,0:T(8,128)(2,1)}, u32[]{:S(2)}) copy-start(bf16[1,512,137]{1,2,0:T(8,128)(2,1)} %param.18) | copy-start | bytes 420868
  5.6 1.8 %copy-start.8 = (bf16[1,137]{1,0:T(2,128)(2,1)S(1)}, bf16[1,137]{1,0:T(2,128)(2,1)}, u32[]{:S(2)}) copy-start(bf16[1,137]{1,0:T(2,128)(2,1)} %param.19) | copy-start | bytes 826
  6.5 1.8 %copy-start = (bf16[192,16,128]{2,1,0:T(8,128)(2,1)S(1)}, bf16[192,16,128]{2,1,0:T(8,128)(2,1)}, u32[]{:S(2)}) copy-start(bf16[192,16,128]{2,1,0:T(8,128)(2,1)} %param.10) | copy-start | bytes 2359300
  63.1 2.6 %copy-start.2 = (bf16[512,137]{1,0:T(8,128)(2,1)S(1)}, bf16[512,137]{1,0:T(8,128)(2,1)}, u32[]{:S(2)}) copy-start(bf16[512,137]{1,0:T(8,128)(2,1)} %get-tuple-element.9) | copy-start | bytes 420868

commit v2 on v1

--- a/solution.py
+++ b/solution.py
@@ -25,35 +25,56 @@
     height = rows - 6
     lane = lax.broadcasted_iota(jnp.int32, (16, breadth), 1)
     taps = k_ref[pl.ds(base, 16), :]
-    acc = [None] * height
-    for col in range(7):
-        shift = col - 3
-        weights = []
-        for row in range(7):
-            t = (6 - row) * 7 + 6 - col if flip else row * 7 + col
-            weights.append(jnp.broadcast_to(taps[:, t : t + 1], (16, breadth)))
-        for r in range(rows):
-            v = x_ref[r, pl.ds(base, 16), :].astype(F32)
-            if shift:
-                edge = h_ref[r, pl.ds(base, 16), :].astype(F32)
-                mask = lane < shift if shift > 0 else lane >= breadth + shift
-                v = pltpu.roll(jnp.where(mask, edge, v), (-shift) % breadth, 1)
+    total = [None] * height
+    for start in range(0, 7, 2):
+        part = [None] * height
+        for col in range(start, min(start + 2, 7)):
+            shift = col - 3
+            weights = []
             for row in range(7):
-                i = r - row
-                if 0 <= i < height:
-                    term = weights[row] * v
-                    acc[i] = term if acc[i] is None else acc[i] + term
-    return acc
-
-
-def prepare(owner_row, owner_col, row0, col0, w_ref, obs_ref, wt_ref, p_ref, pt_ref, obs_slot):
+                t = (6 - row) * 8 + 6 - col if flip else row * 8 + col
+                weights.append(jnp.broadcast_to(taps[:, t : t + 1], (16, breadth)))
+            for r in range(rows):
+                v = x_ref[r, pl.ds(base, 16), :]
+                if shift:
+                    edge = h_ref[r, pl.ds(base, 16), :]
+                    mask = lane < shift if shift > 0 else lane >= breadth + shift
+                    v = pltpu.roll(jnp.where(mask, edge, v), (-shift) % breadth, 1)
+                for row in range(7):
+                    i = r - row
+                    if 0 <= i < height:
+                        term = weights[row] * v
+                        part[i] = term if part[i] is None else part[i] + term
+        for i in range(height):
+            wide = part[i].astype(F32)
+            total[i] = wide if total[i] is None else total[i] + wide
+    return total
+
+
+def prepare(owner, index, weight, obs_t, meta, wt_ref, p_ref, pt_ref, obs_slot):
     height, obs, breadth = wt_ref.shape
     slots = p_ref.shape[0]
     n = slots // CAP
+    si = lax.broadcasted_iota(jnp.int32, (obs, obs), 0)
+    sj = lax.broadcasted_iota(jnp.int32, (obs, obs), 1)
+    earlier = jnp.where(si < sj, 1.0, 0.0).astype(BF)
+    own = owner[...]
+    hot = jnp.where(lax.broadcasted_iota(jnp.int32, (n, obs), 0) == own, 1.0, 0.0)
+    within = jnp.sum(nn(hot.astype(BF), earlier) * hot, axis=0, keepdims=True)
+    slot_row = own * CAP + within.astype(jnp.int32)
+    corner = index[0:1, :].astype(F32)
+    row0 = jnp.floor((corner + 0.5) / breadth)
+    meta[...] = jnp.zeros_like(meta)
+    meta[0:4, :] = weight[...].astype(F32)
+    meta[4:5, :] = row0
+    meta[5:6, :] = corner - row0 * breadth
+    meta[6:7, :] = slot_row.astype(F32)
+    by_obs = meta[...].T
+    w = by_obs[:, 0:4]
+    whole = by_obs.astype(jnp.int32)
     lane = lax.broadcasted_iota(jnp.int32, (obs, breadth), 1)
-    c0 = jnp.broadcast_to(col0[...], (obs, breadth))
-    r0 = jnp.broadcast_to(row0[...], (obs, breadth))
-    w = w_ref[...].astype(F32)
+    r0 = jnp.broadcast_to(whole[:, 4:5], (obs, breadth))
+    c0 = jnp.broadcast_to(whole[:, 5:6], (obs, breadth))
     zero = jnp.zeros((obs, breadth), F32)
     first = lane == c0
     second = lane == c0 + 1
@@ -61,24 +82,12 @@
     bottom = jnp.where(first, w[:, 2:3], jnp.where(second, w[:, 3:4], zero))
     for r in range(height):
         wt_ref[r] = jnp.where(r0 == r, top, jnp.where(r0 == r - 1, bottom, zero)).astype(BF)
-    si = lax.broadcasted_iota(jnp.int32, (obs, obs), 0)
-    sj = lax.broadcasted_iota(jnp.int32, (obs, obs), 1)
-    ones_u = jnp.where(si < sj, 1.0, 0.0).astype(BF)
-    ones_l = jnp.where(sj < si, 1.0, 0.0).astype(BF)
-    own = owner_row[...]
-    hot = jnp.where(lax.broadcasted_iota(jnp.int32, (n, obs), 0) == own, 1.0, 0.0)
-    within = jnp.sum(nn(hot.astype(BF), ones_u) * hot, axis=0, keepdims=True)
-    slot_row = own * CAP + within.astype(jnp.int32)
     place = lax.broadcasted_iota(jnp.int32, (slots, obs), 0) == slot_row
     p = jnp.where(place, 1.0, 0.0).astype(BF)
     p_ref[...] = p
-    own = owner_col[...]
-    hot = jnp.where(lax.broadcasted_iota(jnp.int32, (obs, 128), 1) == own, 1.0, 0.0)
-    within = jnp.sum(nn(ones_l, hot.astype(BF)) * hot, axis=1, keepdims=True)
-    slot_col = own * CAP + within.astype(jnp.int32)
-    place = lax.broadcasted_iota(jnp.int32, (obs, slots), 1) == slot_col
+    place = lax.broadcasted_iota(jnp.int32, (obs, slots), 1) == whole[:, 6:7]
     pt_ref[...] = jnp.where(place, 1.0, 0.0).astype(BF)
-    obs_slot[...] = nn(p, obs_ref[...]).astype(BF)
+    obs_slot[...] = nt(p, obs_t[...]).astype(BF)
 
 
 def remote(src, dst, send, recv, device):
@@ -128,48 +137,45 @@
     return lat > 0, lat < lats - 1, up, down, side
 
 
-def start_exchange(src, off, x, edge, right_in, left_in, send, recv, lats, lons):
+def make_edges(src, edge):
+    pick = selector(src.shape[2])
+
+    def row(r, carry):
+        edge[r] = nt(pick, src[3 + r]).astype(BF)
+        return carry
+
+    lax.fori_loop(0, edge.shape[0], row, 0, unroll=4)
+
+
+def start_exchange(x, edge, right_in, left_in, send, recv, lats, lons):
     height = edge.shape[0]
-    pick = selector(x.shape[2])
     has_up, has_down, up, down, side = copies(
-        src, off, x, edge, right_in, left_in, send, recv, lats, lons
+        x, 3, x, edge, right_in, left_in, send, recv, lats, lons
     )
-    pl.when(has_up)(lambda: up[0].start())
-    pl.when(has_down)(lambda: down[0].start())
-
-    def row(r, carry):
-        edge[r] = nt(pick, src[off + r]).astype(BF)
-        return carry
-
-    lax.fori_loop(0, height, row, 0, unroll=4)
+
+    @pl.when(has_up)
+    def _():
+        for copy in up:
+            copy.start()
+
+    @pl.when(has_down)
+    def _():
+        for copy in down:
+            copy.start()
+
     for copy in side:
         copy.start()
-
-    @pl.when(has_up)
-    def _():
-        up[1].start()
-        up[2].start()
-
-    @pl.when(has_down)
-    def _():
-        down[1].start()
-        down[2].start()
-
-    for missing, at in ((lat_first(has_up), 0), (lat_first(has_down), height + 3)):
-
-        @pl.when(missing)
+    for has, at in ((has_up, 0), (has_down, height + 3)):
+
+        @pl.when(jnp.logical_not(has))
         def _():
             for ref in (x, right_in, left_in):
                 ref[at : at + 3] = jnp.zeros((3,) + ref.shape[1:], BF)
 
 
-def lat_first(has):
-    return jnp.logical_not(has)
-
-
-def end_exchange(src, off, x, edge, right_in, left_in, halo, send, recv, lats, lons):
+def end_exchange(x, edge, right_in, left_in, halo, send, recv, lats, lons):
     has_up, has_down, up, down, side = copies(
-        src, off, x, edge, right_in, left_in, send, recv, lats, lons
+        x, 3, x, edge, right_in, left_in, send, recv, lats, lons
     )
 
     @pl.when(has_up)
@@ -203,20 +209,24 @@
     lats,
     lons,
     state,
-    op_ref,
-    owner_row,
-    owner_col,
-    row0,
-    col0,
-    w_ref,
-    obs_ref,
+    hw_ref,
+    lw_ref,
+    err_ref,
+    owner,
+    index,
+    weight,
+    obs_t,
     k_ref,
-    pwt_ref,
     pw_ref,
     out_ref,
     dep_ref,
     x1,
     x2,
+    stage,
+    meta,
+    tap_rows,
+    taps,
+    pwt,
     halo,
     edge,
     right_in,
@@ -237,8 +247,9 @@
     op_send,
     op_recv,
 ):
-    height, channels, breadth = state.shape
-    levels = obs_ref.shape[1]
+    channels, height, breadth = state.shape
+    levels = obs_t.shape[0]
+    err_row = ops.shape[1] - 16
     lat, lon = lax.axis_index("lat"), lax.axis_index("lon")
     partner = lon + 1 - 2 * lax.rem(lon, 2)
     other = lax.rem(lon + lons - 1 + 2 * lax.rem(lon, 2), lons)
@@ -267,27 +278,44 @@
         for b in (partner, lon, other):
             greet(lat + 1, b)
 
+    def turn(g, carry):
+        at = pl.ds(pl.multiple_of(g * 16, 16), 16)
+        stage[...] = state[at].astype(F32)
+        for r in range(height):
+            x1[3 + r, at, :] = stage[:, r, :].astype(BF)
+        return carry
+
+    lax.fori_loop(0, channels // 16, turn, 0)
+
+    def wires(k):
+        return edge.at[k], right_in.at[k], left_in.at[k]
+
+    make_edges(x1, edge.at[0])
+    ops[lon] = jnp.zeros(ops.shape[1:], BF)
+    ops[lon, :channels, :] = hw_ref[0]
+    ops[lon, channels : channels + levels, :] = lw_ref[0]
+    ops[lon, err_row : err_row + 1, :levels] = err_ref[...]
     sides = lax.min(lat, 1) + lax.min(lats - 1 - lat, 1)
     pl.semaphore_wait(barrier, half + 1 + 3 * sides)
-
-    def wires(k):
-        return edge.at[k], right_in.at[k], left_in.at[k]
-
-    start_exchange(state, 0, x1, *wires(0), send.at[0], recv.at[0], lats, lons)
+    start_exchange(x1, *wires(0), send.at[0], recv.at[0], lats, lons)
+    mine = ops.at[lon]
     sends = [
-        remote(op_ref, ops.at[lon], op_send.at[j], op_recv.at[lon], {"lat": lat, "lon": b})
+        remote(mine, mine, op_send.at[j], op_recv.at[lon], {"lat": lat, "lon": b})
         for j, b in enumerate([partner] + peers)
     ]
     for copy in sends:
         copy.start()
-    x1[3 : 3 + height] = state[...]
-    ops[lon] = op_ref[...]
-    prepare(owner_row, owner_col, row0, col0, w_ref, obs_ref, wt, p_mat, pt_mat, obs_slot)
-    end_exchange(state, 0, x1, *wires(0), halo, send.at[0], recv.at[0], lats, lons)
+    tap_rows[...] = jnp.zeros_like(tap_rows)
+    for row in range(7):
+        tap_rows[8 * row : 8 * row + 7, :] = k_ref[row].astype(F32)
+    taps[...] = tap_rows[...].T.astype(BF)
+    pwt[...] = pw_ref[...].astype(F32).T.astype(BF)
+    prepare(owner, index, weight, obs_t, meta, wt, p_mat, pt_mat, obs_slot)
+    end_exchange(x1, *wires(0), halo, send.at[0], recv.at[0], lats, lons)
 
     def group(g, carry):
         base = pl.multiple_of(g * 16, 16)
-        for i, v in enumerate(conv_group(x1, halo, k_ref, base, False)):
+        for i, v in enumerate(conv_group(x1, halo, taps, base, False)):
             mixed[i, pl.ds(base, 16), :] = v.astype(BF)
         return carry
 
@@ -307,14 +335,14 @@
 
     def ahead(q, carry):
         r = q * 2
-        pre = nn(pwt_ref[...], jnp.concatenate([mixed[r], mixed[r + 1]], axis=1))
+        pre = nn(pwt[...], jnp.concatenate([mixed[r], mixed[r + 1]], axis=1))
         square = pre * pre
         t = jnp.tanh(a * (pre + c3 * (square * pre)))
         gate = 0.5 * (1.0 + t)
         slope = gate + (0.5 * pre) * (1.0 - t * t) * (a * (1.0 + (3.0 * c3) * square))
         grid_f[r] = slope[:, :breadth]
         grid_f[r + 1] = slope[:, breadth:]
-        here = jnp.concatenate([state[r], state[r + 1]], axis=1).astype(F32)
+        here = jnp.concatenate([x1[r + 3], x1[r + 4]], axis=1).astype(F32)
         analysis = (here + pre * gate).astype(BF)
         total[...] += nt(jnp.concatenate([wt[r], wt[r + 1]], axis=1), analysis)
         return carry
@@ -327,7 +355,6 @@
         remote(
             ops.at[b], ops.at[b], op_send.at[0], op_recv.at[b], {"lat": lat, "lon": partner}
         ).wait_recv()
-    err_row = op_ref.shape[0] - 16
 
     def instrument(o, carry):
         at = pl.ds(pl.multiple_of(o * CAP, CAP), CAP)
@@ -342,7 +369,7 @@
         return carry
 
     lax.fori_loop(0, lons, instrument, 0, unroll=4)
-    dep_ref[...] = nn(pt_mat[...], mis[...]).astype(BF)
+    dep_ref[...] = nn(pt_mat[...], mis[...]).T.astype(BF)
     adj_t = nn(pt_mat[...], adj[...]).T.astype(BF)
 
     def behind(q, carry):
@@ -359,13 +386,15 @@
     lax.fori_loop(0, height // 2, behind, 0)
     for copy in sends + forwards:
         copy.wait_send()
-    start_exchange(x2, 3, x2, *wires(1), send.at[1], recv.at[1], lats, lons)
-    end_exchange(x2, 3, x2, *wires(1), halo, send.at[1], recv.at[1], lats, lons)
+    make_edges(x2, edge.at[1])
+    start_exchange(x2, *wires(1), send.at[1], recv.at[1], lats, lons)
+    end_exchange(x2, *wires(1), halo, send.at[1], recv.at[1], lats, lons)
 
     def group_back(g, carry):
         base = pl.multiple_of(g * 16, 16)
-        for i, v in enumerate(conv_group(x2, halo, k_ref, base, True)):
-            out_ref[i, pl.ds(base, 16), :] = (v + grid_f[i, pl.ds(base, 16), :]).astype(BF)
+        for i, v in enumerate(conv_group(x2, halo, taps, base, True)):
+            stage[:, i, :] = v + grid_f[i, pl.ds(base, 16), :]
+        out_ref[pl.ds(base, 16)] = stage[...].astype(BF)
         return carry
 
     lax.fori_loop(0, channels // 16, group_back, 0)
@@ -388,29 +417,17 @@
     hid = hidden_weight.shape[2]
     lats, n = lax.axis_size("lat"), lax.axis_size("lon")
     slots = n * CAP
-    fill = (-(channels + levels)) % 16
-    pack = jnp.concatenate(
-        [
-            hidden_weight[0],
-            jnp.pad(level_weight[0].T, ((0, fill), (0, 0))),
-            jnp.pad(inverse_error, ((0, 15), (0, hid - levels))),
-        ],
-        axis=0,
-    )
-    taps = jnp.pad(depth_kernel.reshape(channels, 49).astype(F32), ((0, 0), (0, 79)))
-    row0 = column_index[:, :1] // breadth
-    col0 = column_index[:, :1] - row0 * breadth
+    depth = channels + levels + (-(channels + levels)) % 16 + 16
     args = (
-        state.transpose(1, 0, 2),
-        pack,
-        owner.reshape(1, obs),
-        owner,
-        row0,
-        col0,
-        column_weight,
-        observed,
-        taps,
-        point_weight.T,
+        state,
+        hidden_weight,
+        level_weight.transpose(0, 2, 1),
+        inverse_error,
+        owner.T,
+        column_index.T,
+        column_weight.T,
+        observed.T,
+        depth_kernel.transpose(1, 2, 0),
         point_weight,
     )
     rows = height + 6
@@ -419,19 +436,24 @@
     grad, departures = pl.pallas_call(
         lambda *refs: kernel(lats, n, *refs),
         out_shape=(
-            jax.ShapeDtypeStruct((height, channels, breadth), BF),
-            jax.ShapeDtypeStruct((obs, levels), BF),
+            jax.ShapeDtypeStruct((channels, height, breadth), BF),
+            jax.ShapeDtypeStruct((levels, obs), BF),
         ),
         in_specs=[VM] * len(args),
         out_specs=(VM, VM),
         scratch_shapes=[
             vm(grid, BF),
             vm(grid, BF),
+            vm((16, height, breadth), F32),
+            vm((8, obs), F32),
+            vm((64, channels), F32),
+            vm((channels, 64), BF),
+            vm((channels, channels), BF),
             vm(grid, BF),
             vm((2, height, 8, channels), BF),
             vm((2, rows, 8, channels), BF),
             vm((2, rows, 8, channels), BF),
-            vm((n,) + pack.shape, BF),
+            vm((n, depth, hid), BF),
             vm((height, obs, breadth), BF),
             vm((slots, obs), BF),
             vm((obs, slots), BF),
@@ -451,7 +473,7 @@
             vmem_limit_bytes=56 << 20, collective_id=0, has_side_effects=True
         ),
     )(*args)
-    return (grad.transpose(1, 0, 2), departures)
+    return (grad, departures.T)
 
 
 def solution(mesh):

time: 67.7 us -> 59.1 us (0.87); the launches traced: 66.4 us -> 58.5 us
  local copies, waits for them, and re-layouts: 9.64 us -> 2.85 us
  other arithmetic: 2.39 us -> 0 us
  Pallas kernels: 53.7 us -> 55 us
    unnamed x26 -> x4, local copies, waits for them, and re-layouts: 8.75 us -> 2.85 us
    pallas_call x1, Pallas kernels: 53.7 us -> 55 us  [body(): pl.pallas_call(lambda *refs: kernel(lats, n, *refs), out_shape=(jax.Shape...]
    sub x1 -> x0, other arithmetic: 0.96 us -> none  [body(): col0 = column_index[:, :1] - row0 * breadth]
    convert_element_type x2 -> x0, local copies, waits for them, and re-layouts: 0.89 us -> none  [body(): depth_kernel.reshape(channels, 49).astype(F32)]
    concatenate x1 -> x0, other arithmetic: 0.78 us -> none  [body(): jnp.concatenate([hidden_weight[0], jnp.pad(level_weight[0].T, ((0, fill),...]
where the time goes in v2:
time: 59.1 us; the launch traced here: 58.5 us
  Pallas kernels  55 us (93%)
  local copies, waits for them, and re-layouts  2.85 us (5%)
  between operations  0.65 us (1%)
    pallas_call x1, Pallas kernels, body(): pl.pallas_call(lambda *refs: kernel(lats, n, *refs), out_shape=(jax.Shape...  55 us
    unnamed x4, local copies, waits for them, and re-layouts  2.85 us

profile of v2, /device:TPU:0, one launch (start us, length us, event | category | flops | bytes accessed | tf_op | source)
XLA Modules:
  0.0 58.5 jit_solution(2080447441621927979)
XLA Ops:
  0.6 55.0 %shard_map.113 = (bf16[192,16,128]{2,1,0:T(8,128)(2,1)}, bf16[137,512]{1,0:T(8,128)(2,1)}) custom-call(bf16[192,16,128]{2,1,0:T(8,128)(2,1)} %refs_0_.1, bf16[1,192,512]{2,1,0:T(8,128)(2,1)} %refs_1_.1, bf16[1,137,512]{2,1,0:T(8,128)(2,1)} %bitcast.7, bf16[1,137]{1,0:T(2,128)(2,1)} %refs_3_.1, s32[1,512]{1,0:T(1,128)} %bitcast.13, s32[4,512]{1,0:T(4,128)} %bitcast.11, ...), custom_call_target="tpu_custom_call" | custom-call | tf_op jit(solution)/shard_map/pallas_call | solution.py:436
  55.7 0.0 copy-start
  55.7 2.2 %copy.14 = bf16[192,16,128]{2,1,0:T(8,128)(2,1)} copy(bf16[192,16,128]{2,1,0:T(8,128)(2,1)} %get-tuple-element.8) | data formatting | bytes 1572864
  57.9 0.0 copy-done
  57.9 0.7 %copy.15 = bf16[512,137]{0,1:T(8,128)(2,1)} copy(bf16[512,137]{0,1:T(8,128)(2,1)S(1)} %bitcast.9) | data formatting | bytes 280576
Async XLA Ops:
  55.7 2.2 %copy-start = (bf16[137,512]{1,0:T(8,128)(2,1)S(1)}, bf16[137,512]{1,0:T(8,128)(2,1)}, u32[]{:S(2)}) copy-start(bf16[137,512]{1,0:T(8,128)(2,1)} %get-tuple-element.5) | copy-start | bytes 420868

commit v3 on v2

--- a/solution.py
+++ b/solution.py
@@ -25,30 +25,25 @@
     height = rows - 6
     lane = lax.broadcasted_iota(jnp.int32, (16, breadth), 1)
     taps = k_ref[pl.ds(base, 16), :]
-    total = [None] * height
-    for start in range(0, 7, 2):
-        part = [None] * height
-        for col in range(start, min(start + 2, 7)):
-            shift = col - 3
-            weights = []
+    acc = [None] * height
+    for col in range(7):
+        shift = col - 3
+        weights = []
+        for row in range(7):
+            t = (6 - row) * 8 + 6 - col if flip else row * 8 + col
+            weights.append(jnp.broadcast_to(taps[:, t : t + 1], (16, breadth)))
+        for r in range(rows):
+            v = x_ref[r, pl.ds(base, 16), :].astype(F32)
+            if shift:
+                edge = h_ref[r, pl.ds(base, 16), :].astype(F32)
+                mask = lane < shift if shift > 0 else lane >= breadth + shift
+                v = pltpu.roll(jnp.where(mask, edge, v), (-shift) % breadth, 1)
             for row in range(7):
-                t = (6 - row) * 8 + 6 - col if flip else row * 8 + col
-                weights.append(jnp.broadcast_to(taps[:, t : t + 1], (16, breadth)))
-            for r in range(rows):
-                v = x_ref[r, pl.ds(base, 16), :]
-                if shift:
-                    edge = h_ref[r, pl.ds(base, 16), :]
-                    mask = lane < shift if shift > 0 else lane >= breadth + shift
-                    v = pltpu.roll(jnp.where(mask, edge, v), (-shift) % breadth, 1)
-                for row in range(7):
-                    i = r - row
-                    if 0 <= i < height:
-                        term = weights[row] * v
-                        part[i] = term if part[i] is None else part[i] + term
-        for i in range(height):
-            wide = part[i].astype(F32)
-            total[i] = wide if total[i] is None else total[i] + wide
-    return total
+                i = r - row
+                if 0 <= i < height:
+                    term = weights[row] * v
+                    acc[i] = term if acc[i] is None else acc[i] + term
+    return acc
 
 
 def prepare(owner, index, weight, obs_t, meta, wt_ref, p_ref, pt_ref, obs_slot):
@@ -308,7 +303,7 @@
     tap_rows[...] = jnp.zeros_like(tap_rows)
     for row in range(7):
         tap_rows[8 * row : 8 * row + 7, :] = k_ref[row].astype(F32)
-    taps[...] = tap_rows[...].T.astype(BF)
+    taps[...] = tap_rows[...].T
     pwt[...] = pw_ref[...].astype(F32).T.astype(BF)
     prepare(owner, index, weight, obs_t, meta, wt, p_mat, pt_mat, obs_slot)
     end_exchange(x1, *wires(0), halo, send.at[0], recv.at[0], lats, lons)
@@ -447,7 +442,7 @@
             vm((16, height, breadth), F32),
             vm((8, obs), F32),
             vm((64, channels), F32),
-            vm((channels, 64), BF),
+            vm((channels, 64), F32),
             vm((channels, channels), BF),
             vm(grid, BF),
             vm((2, height, 8, channels), BF),

time: 59.1 us -> 58.4 us (0.988)
  Pallas kernels: 55 us -> 54.3 us
    pallas_call x1, Pallas kernels: 55 us -> 54.3 us  [body(): pl.pallas_call(lambda *refs: kernel(lats, n, *refs), out_shape=(jax.Shape...]
where the time goes in v3:
time: 58.4 us; the launch traced here: 57.8 us
  Pallas kernels  54.3 us (93%)
  local copies, waits for them, and re-layouts  2.85 us (5%)
  between operations  0.65 us (1%)
    pallas_call x1, Pallas kernels, body(): pl.pallas_call(lambda *refs: kernel(lats, n, *refs), out_shape=(jax.Shape...  54.3 us
    unnamed x4, local copies, waits for them, and re-layouts  2.85 us

profile of v3, /device:TPU:0, one launch (start us, length us, event | category | flops | bytes accessed | tf_op | source)
XLA Modules:
  0.0 57.8 jit_solution(12592242751947015390)
XLA Ops:
  0.6 54.3 %shard_map.113 = (bf16[192,16,128]{2,1,0:T(8,128)(2,1)}, bf16[137,512]{1,0:T(8,128)(2,1)}) custom-call(bf16[192,16,128]{2,1,0:T(8,128)(2,1)} %refs_0_.1, bf16[1,192,512]{2,1,0:T(8,128)(2,1)} %refs_1_.1, bf16[1,137,512]{2,1,0:T(8,128)(2,1)} %bitcast.7, bf16[1,137]{1,0:T(2,128)(2,1)} %refs_3_.1, s32[1,512]{1,0:T(1,128)} %bitcast.13, s32[4,512]{1,0:T(4,128)} %bitcast.11, ...), custom_call_target="tpu_custom_call" | custom-call | tf_op jit(solution)/shard_map/pallas_call | solution.py:431
  55.0 0.0 copy-start
  55.0 2.2 %copy.14 = bf16[192,16,128]{2,1,0:T(8,128)(2,1)} copy(bf16[192,16,128]{2,1,0:T(8,128)(2,1)} %get-tuple-element.8) | data formatting | bytes 1572864
  57.2 0.0 copy-done
  57.2 0.7 %copy.15 = bf16[512,137]{0,1:T(8,128)(2,1)} copy(bf16[512,137]{0,1:T(8,128)(2,1)S(1)} %bitcast.9) | data formatting | bytes 280576
Async XLA Ops:
  55.0 2.2 %copy-start = (bf16[137,512]{1,0:T(8,128)(2,1)S(1)}, bf16[137,512]{1,0:T(8,128)(2,1)}, u32[]{:S(2)}) copy-start(bf16[137,512]{1,0:T(8,128)(2,1)} %get-tuple-element.5) | copy-start | bytes 420868
